TPU v7x, 32 devices: a whole 2x2x4 slice. The times are simulated.
32 devices in a mesh: groups: 2 (over x), seq: 8 (over z, y), head: 2 (over core).
Axes of the slice: x: 2, y: 2, z: 4, core: 2. Of those that a mesh axis runs over, the one named last changes fastest.
Arguments:
- query_proj: bfloat16 [4096, 2048], P(('groups', 'seq'), 'head'), parts along dimension 0, may hold values from -6 to 6
- key_proj: bfloat16 [4096, 2048], P(('groups', 'seq'), 'head'), parts along dimension 0, may hold values from -6 to 6
- value_proj: bfloat16 [4096, 2048], P(('groups', 'seq'), 'head'), parts along dimension 0, may hold values from -6 to 6
- segment_ids: int32 [4096], P(('groups', 'seq')), parts along dimension 0, may hold values from 0 to 5, never falling along the last dimension, each value on 1 to 682 neighbouring positions
- feature_map: bfloat16 [16, 128, 256], P('head'), may hold values from -0.5 to 0.5
- head_gain: float32 [2048], P('head'), may hold values from 0.1 to 1.9
- residual: bfloat16 [4096, 2048], P(('groups', 'seq', 'head')), parts along dimension 0, may hold values from -6 to 6
- out_weight: bfloat16 [2048, 2048], P('head'), may hold values from -0.125 to 0.125
- norm_gain: float32 [2048], replicated, may hold values from 0.1 to 1.9
- router: bfloat16 [2048, 16], replicated, may hold values from -0.125 to 0.125
- w_gate: bfloat16 [16, 2048, 1024], P(('seq', 'head')), may hold values from -0.125 to 0.125
- w_up: bfloat16 [16, 2048, 1024], P(('seq', 'head')), may hold values from -0.125 to 0.125
- w_down: bfloat16 [16, 1024, 2048], P(('seq', 'head')), may hold values from -0.1875 to 0.1875
- expert_ids: int32 [4096, 8], P(('groups', 'seq', 'head')), parts along dimension 0, may hold values from 0 to 15, all different within a row; in each aligned block of 128 rows (0 to 127, 128 to 255, ...) at most 80 rows name the same one
Outputs:
- hidden: bfloat16 [4096, 2048], P(('groups', 'seq', 'head')), parts along dimension 0
- expert_sum: bfloat16 [4096, 2048], P(('groups', 'seq', 'head')), parts along dimension 0
There are 2 independent parts, one for each index of `groups`. A program takes and returns all parts, laid end to end along the dimension named above; an argument that names none is the same for every part. Nothing has to cross between parts.
Inputs may be any that keep to these rules, and one draw needn't show every extreme that they name: `segment_ids`: segment ids never fall; every segment has 1 to 682 tokens, one exactly 682. `expert_ids`: A token's 8 experts differ. In the 128 rows of one device (aligned blocks of rows) no expert is named more than 80 times, and in some such block some expert is named exactly 80 times.
All inputs are finite; a program needn't handle non-finite values.
Results may differ from a plain program's by a relative error of at most 0.011.
Values may be sent and summed in bfloat16 or wider, within the bound.
A program may use at most 128 MiB of HBM per device.

v0:
```python
import jax
import jax.numpy as jnp
from jax import lax
from jax.sharding import PartitionSpec as P


def carried_in(last_seg, local_state, token_count):
    place = lax.axis_index("seq")
    blocks = lax.axis_size("seq")
    longest = token_count * blocks // 3
    reach = min(blocks - 1, max(1, (longest - 2) // token_count + 1))
    last_all = lax.all_gather(last_seg, "seq")

    def last_of(back):
        index = place - back
        return jnp.where(index >= 0, last_all[jnp.maximum(index, 0)], -1 - back)

    before = last_of(1)
    carried = None
    window = local_state
    span = 1
    covered = 0
    while covered < reach:
        shifted = lax.ppermute(
            window.astype(jnp.bfloat16), "seq", [(i, i + span) for i in range(blocks - span)]
        ).astype(jnp.float32)
        if carried is None:
            carried = shifted
        else:
            carried = carried + jnp.where(last_of(span) == before, shifted, 0.0)
        covered += span
        if covered < reach:
            window = window + jnp.where(last_of(span) == last_seg, shifted, 0.0)
        span *= 2
    return (before, carried)


def features_of(inputs, feature_map, head_count, head_dim):
    grouped = inputs.reshape(inputs.shape[0], head_count, head_dim)
    projected = jnp.einsum("thd,hdf->thf", grouped, feature_map, preferred_element_type=jnp.float32)
    return (jax.nn.elu(projected) + 1.0).astype(jnp.bfloat16)


def run_expert(rows, gate, w_gate, w_up, w_down):
    gate_pre = jnp.dot(rows, w_gate, preferred_element_type=jnp.float32)
    up_pre = jnp.dot(rows, w_up, preferred_element_type=jnp.float32)
    activated = (jax.nn.silu(gate_pre) * up_pre).astype(jnp.bfloat16)
    answer = jnp.dot(activated, w_down, preferred_element_type=jnp.float32)
    return answer * gate[:, None]


def shards(
    query_proj,
    key_proj,
    value_proj,
    segment_ids,
    feature_map,
    head_gain,
    residual,
    out_weight,
    norm_gain,
    router,
    w_gate,
    w_up,
    w_down,
    expert_ids,
):
    token_count = query_proj.shape[0]
    head_count = feature_map.shape[0]
    head_dim = feature_map.shape[1]
    query_feat = features_of(query_proj, feature_map, head_count, head_dim)
    key_feat = features_of(key_proj, feature_map, head_count, head_dim)
    values = value_proj.reshape(token_count, head_count, head_dim)
    last_seg = segment_ids[token_count - 1]
    tail_mask = (segment_ids == last_seg).astype(jnp.bfloat16)
    local_state = jnp.einsum(
        "thf,thd->hfd",
        key_feat * tail_mask[:, None, None],
        values,
        preferred_element_type=jnp.float32,
    )
    seg_before, state_before = carried_in(last_seg, local_state, token_count)
    scores = jnp.einsum("thf,shf->hts", query_feat, key_feat, preferred_element_type=jnp.float32)
    positions = lax.iota(jnp.int32, token_count)
    allowed = (positions[None, :] <= positions[:, None]) & (
        segment_ids[None, :] == segment_ids[:, None]
    )
    block_weights = jnp.where(allowed[None], scores, 0.0).astype(jnp.bfloat16)
    within = jnp.einsum("hts,shd->thd", block_weights, values, preferred_element_type=jnp.float32)
    carried = jnp.einsum(
        "thf,hfd->thd",
        query_feat,
        state_before.astype(jnp.bfloat16),
        preferred_element_type=jnp.float32,
    )
    carry_mask = (segment_ids == seg_before).astype(jnp.float32)
    mixed = within + carry_mask[:, None, None] * carried
    scale = lax.rsqrt(jnp.mean(mixed * mixed, axis=2, keepdims=True) + 1e-06)
    attn_heads = (
        (mixed * scale * head_gain.reshape(head_count, head_dim))
        .reshape(token_count, head_count * head_dim)
        .astype(jnp.bfloat16)
    )
    attn_rows = lax.all_to_all(attn_heads, "head", split_axis=0, concat_axis=1, tiled=True)
    projected = jnp.dot(
        attn_rows,
        lax.all_gather(out_weight, "head", axis=0, tiled=True),
        preferred_element_type=jnp.float32,
    )
    hidden = (residual.astype(jnp.float32) + projected).astype(jnp.bfloat16)
    hidden_f = hidden.astype(jnp.float32)
    normed = (
        hidden_f
        * lax.rsqrt(jnp.mean(hidden_f * hidden_f, axis=1, keepdims=True) + 1e-05)
        * norm_gain
    ).astype(jnp.bfloat16)
    logits = jnp.dot(normed, router, preferred_element_type=jnp.float32)
    expert_count = router.shape[1]
    expert_iota = lax.iota(jnp.int32, expert_count)
    picked = expert_ids[:, :, None] == expert_iota[None, None, :]
    chosen = jnp.sum(jnp.where(picked, logits[:, None, :], 0.0), axis=2)
    gates = jax.nn.sigmoid(chosen)
    gate_weights = gates / jnp.sum(gates, axis=1, keepdims=True)
    dense_gates = jnp.sum(jnp.where(picked, gate_weights[:, :, None], 0.0), axis=1)
    spread = ("seq", "head")
    all_rows = lax.all_gather(normed, spread, axis=0, tiled=True)
    all_gates = lax.all_gather(dense_gates, spread, axis=0, tiled=True)
    exp_dev = w_gate.shape[0]
    first = (lax.axis_index("seq") * lax.axis_size("head") + lax.axis_index("head")) * exp_dev
    partial = 0.0
    for own in range(exp_dev):
        gate = jnp.sum(jnp.where(expert_iota[None, :] == first + own, all_gates, 0.0), axis=1)
        partial = partial + run_expert(all_rows, gate, w_gate[own], w_up[own], w_down[own])
    expert_sum = lax.psum_scatter(
        partial.astype(jnp.bfloat16), spread, scatter_dimension=0, tiled=True
    )
    return (hidden, expert_sum)


def solution(mesh):
    placed = (
        P(("groups", "seq"), "head"),
        P(("groups", "seq"), "head"),
        P(("groups", "seq"), "head"),
        P(("groups", "seq")),
        P("head", None, None),
        P("head"),
        P(("groups", "seq", "head"), None),
        P("head", None),
        P(),
        P(),
        P(("seq", "head"), None, None),
        P(("seq", "head"), None, None),
        P(("seq", "head"), None, None),
        P(("groups", "seq", "head"), None),
    )
    return jax.shard_map(
        shards,
        mesh=mesh,
        in_specs=placed,
        out_specs=(P(("groups", "seq", "head"), None), P(("groups", "seq", "head"), None)),
        check_vma=False,
    )
```

profile of v0, /device:TPU:0, one launch (start us, length us, event | category | flops | bytes accessed | tf_op | source)
XLA Modules:
  0.0 290.1 jit_solution(12551976899202699490)
XLA Ops:
  7.3 0.7 all-gather.3.cloned.1.call-update
  8.6 1.2 slice_dynamic-update-slice_fusion
  9.9 13.1 %all-reduce = s32[8]{0:T(128)S(1)} all-reduce(s32[8]{0:T(128)S(1)} %get-tuple-element.4), channel_id=1, replica_groups=mesh['groups'=2,'seq'=8,'head'=2] {'seq'}, use_global_device_ids=true, to_apply=%add | all-reduce | flops 8 | bytes 64
  22.9 0.6 fusion.43
  24.2 0.7 compare_convert_fusion.1
  24.9 1.1 fusion.12
  26.1 1.2 fusion.44
  27.3 3.4 %collective-permute-start = (bf16[8,256,128]{2,1,0:T(8,128)(2,1)}, bf16[8,256,128]{2,1,0:T(8,128)(2,1)S(1)}, u32[]{:S(2)}, u32[]{:S(2)}) collective-permute-start(bf16[8,256,128]{2,1,0:T(8,128)(2,1)} %get-tuple-element.8), channel_id=1, source_target_pairs={{0,2},{2,4},{4,6},{6,8},{8,10},{10,12},{12,14},{1,3},{3,5},{5,7},{... | collective-permute-start | bytes 1572872 | tf_op jit(solution)/shard_map/ppermute | solution.py:24
  31.4 7.9 %collective-permute-done = bf16[8,256,128]{2,1,0:T(8,128)(2,1)S(1)} collective-permute-done((bf16[8,256,128]{2,1,0:T(8,128)(2,1)}, bf16[8,256,128]{2,1,0:T(8,128)(2,1)S(1)}, u32[]{:S(2)}, u32[]{:S(2)}) %collective-permute-start) | collective-permute-done | bytes 524320 | tf_op jit(solution)/shard_map/ppermute | solution.py:24
  39.3 0.9 fusion.18
  40.2 4.4 %collective-permute-start.1 = (bf16[8,256,128]{2,1,0:T(8,128)(2,1)}, bf16[8,256,128]{2,1,0:T(8,128)(2,1)S(1)}, u32[]{:S(2)}, u32[]{:S(2)}) collective-permute-start(bf16[8,256,128]{2,1,0:T(8,128)(2,1)} %fusion.18), channel_id=1, source_target_pairs={{0,4},{2,6},{4,8},{6,10},{8,12},{10,14},{1,5},{3,7},{5,9},{7,11},{... | collective-permute-start | bytes 1572872 | tf_op jit(solution)/shard_map/ppermute | solution.py:24
  45.4 2.2 fusion.9
  47.6 5.0 %collective-permute-done.1 = bf16[8,256,128]{2,1,0:T(8,128)(2,1)S(1)} collective-permute-done((bf16[8,256,128]{2,1,0:T(8,128)(2,1)}, bf16[8,256,128]{2,1,0:T(8,128)(2,1)S(1)}, u32[]{:S(2)}, u32[]{:S(2)}) %collective-permute-start.1) | collective-permute-done | bytes 524320 | tf_op jit(solution)/shard_map/ppermute | solution.py:24
  52.6 1.4 fusion.16
  54.0 2.5 multiply_reduce_fusion
  57.0 4.2 %all_to_all.16 = bf16[2,128,1024]{1,2,0:T(8,128)(2,1)S(1)} all-to-all(bf16[2,128,1024]{1,2,0:T(8,128)(2,1)S(1)} %copy.47), channel_id=1, replica_groups=mesh['groups'=2,'seq'=8,'head'=2] {'head'}, dimensions={0} | all-to-all | bytes 1048576 | tf_op jit(solution)/shard_map/all_to_all | solution.py:104
  61.2 4.8 %fusion.20 = (f32[128]{0:T(128)S(1)}, bf16[128,2048]{1,0:T(8,128)(2,1)S(1)}) fusion(bf16[128,2048]{0,1:T(8,128)(2,1)S(1)} %bitcast.71, bf16[2048,2048]{1,0:T(8,128)(2,1)} %all-gather.3.cloned.1.call-done, bf16[128,2048]{1,0:T(8,128)(2,1)S(1)} %copy-done.3), kind=kOutput, calls=%fused_computation.32 | convolution fusion | flops 1075314560 | bytes 9961984 | tf_op jit(solution)/shard_map/dot_general | solution.py:105
  66.0 1.0 fusion.22
  67.1 1.3 fusion.45
  68.5 20.6 %all_gather.15 = f32[2048,16]{0,1:T(8,128)S(1)} all-gather(f32[128,16]{0,1:T(8,128)S(1)} %select_reduce_fusion.1), channel_id=1, replica_groups=mesh['groups'=2,'seq'=8,'head'=2] {'seq','head'}, dimensions={0}, use_global_device_ids=true | all-gather | bytes 139264 | tf_op jit(solution)/shard_map/all_gather | solution.py:127
  89.2 51.7 %all-gather.5.cloned.1.call-done = bf16[2048,2048]{1,0:T(8,128)(2,1)} async-done(((bf16[128,2048]{1,0:T(8,128)(2,1)}), bf16[2048,2048]{1,0:T(8,128)(2,1)}) %all-gather.5.cloned.1.call-update) | async-done | bytes 8388624 | tf_op jit(solution)/shard_map/all_gather | solution.py:126
  140.9 14.4 %fusion.3 = f32[2048,1024]{1,0:T(8,128)} fusion(bf16[2048,2048]{1,0:T(8,128)(2,1)} %all-gather.5.cloned.1.call-done, bf16[1,2048,1024]{2,1,0:T(8,128)(2,1)} %param.24), kind=kOutput, calls=%fused_computation.8 | convolution fusion | flops 8589934592 | bytes 20971520 | tf_op jit(solution)/shard_map/dot_general | solution.py:45
  155.3 26.0 %multiply_convert_fusion = bf16[2048,2048]{1,0:T(8,128)(2,1)} fusion(f32[2048]{0:T(1024)S(1)} %select_reduce_fusion, f32[2048,1024]{1,0:T(8,128)} %fusion.3, bf16[2048,2048]{1,0:T(8,128)(2,1)} %all-gather.5.cloned.1.call-done, bf16[1,1024,2048]{2,1,0:T(8,128)(2,1)} %param.26, bf16[1,2048,1024]{2,1,0:T(8,128)(2,1)} %param.25), kind=kOutput, calls=%fused_computation | convolution fusion | flops 17200840704 | bytes 33562624 | tf_op jit(solution)/shard_map/dot_general | solution.py:48
  181.3 102.2 %reduce-scatter.2.cloned.1.call-done = bf16[128,2048]{1,0:T(8,128)(2,1)} async-done(((bf16[2048,2048]{1,0:T(8,128)(2,1)}), bf16[128,2048]{1,0:T(8,128)(2,1)}) %reduce-scatter.2.cloned.1.call-update) | async-done | bytes 524304 | tf_op jit(solution)/shard_map/reduce_scatter | solution.py:134
  (44 shorter events, 1.5 us)
Async XLA Ops:
  7.2 17.7 %copy-start = (bf16[8,128,256]{2,1,0:T(8,128)(2,1)S(1)}, bf16[8,128,256]{2,1,0:T(8,128)(2,1)}, u32[]{:S(2)}) copy-start(bf16[8,128,256]{2,1,0:T(8,128)(2,1)} %param.18) | copy-start | bytes 1572868
  7.2 0.8 copy-start.11
  7.2 1.4 copy-start.7
  7.2 17.7 %copy-start.10 = (bf16[256,1024]{1,0:T(8,128)(2,1)S(1)}, bf16[256,1024]{1,0:T(8,128)(2,1)}, u32[]{:S(2)}) copy-start(bf16[256,1024]{1,0:T(8,128)(2,1)} %param.15) | copy-start | bytes 1572868
  7.2 18.8 %copy-start.4 = (bf16[256,1024]{1,0:T(8,128)(2,1)S(1)}, bf16[256,1024]{1,0:T(8,128)(2,1)}, u32[]{:S(2)}) copy-start(bf16[256,1024]{1,0:T(8,128)(2,1)} %param.16) | copy-start | bytes 1572868
  7.2 53.9 %all-gather.3.cloned.1.call-start = ((), (), s32[]{:S(2)}) async-start(), calls=%async_computation.2 | async-start | bytes 12582912 | tf_op jit(solution)/shard_map/all_gather | solution.py:107
  8.0 133.0 %all-gather.5.cloned.1.call-start = ((), (), s32[]{:S(2)}) async-start(), calls=%async_computation.3 | async-start | bytes 8912896 | tf_op jit(solution)/shard_map/all_gather | solution.py:126
  27.3 12.0 %collective-permute-start = (bf16[8,256,128]{2,1,0:T(8,128)(2,1)}, bf16[8,256,128]{2,1,0:T(8,128)(2,1)S(1)}, u32[]{:S(2)}, u32[]{:S(2)}) collective-permute-start(bf16[8,256,128]{2,1,0:T(8,128)(2,1)} %get-tuple-element.8), channel_id=1, source_target_pairs={{0,2},{2,4},{4,6},{6,8},{8,10},{10,12},{12,14},{1,3},{3,5},{5,7},{... | collective-permute-start | bytes 1572872 | tf_op jit(solution)/shard_map/ppermute | solution.py:24
  40.2 12.3 %collective-permute-start.1 = (bf16[8,256,128]{2,1,0:T(8,128)(2,1)}, bf16[8,256,128]{2,1,0:T(8,128)(2,1)S(1)}, u32[]{:S(2)}, u32[]{:S(2)}) collective-permute-start(bf16[8,256,128]{2,1,0:T(8,128)(2,1)} %fusion.18), channel_id=1, source_target_pairs={{0,4},{2,6},{4,8},{6,10},{8,12},{10,14},{1,5},{3,7},{5,9},{7,11},{... | collective-permute-start | bytes 1572872 | tf_op jit(solution)/shard_map/ppermute | solution.py:24
  47.5 5.0 %copy-start.2 = (bf16[256,8,256]{0,2,1:T(8,128)(2,1)}, bf16[256,8,256]{0,2,1:T(8,128)(2,1)S(1)}, u32[]{:S(2)}) copy-start(bf16[256,8,256]{0,2,1:T(8,128)(2,1)S(1)} %fusion.9) | copy-start | bytes 3145732
  47.5 9.0 %copy-start.9 = (f32[1024]{0:T(1024)S(1)}, f32[1024]{0:T(1024)}, u32[]{:S(2)}) copy-start(f32[1024]{0:T(1024)} %param.19) | copy-start | bytes 12292
  54.0 7.1 %copy-start.3 = (bf16[128,2048]{1,0:T(8,128)(2,1)S(1)}, bf16[128,2048]{1,0:T(8,128)(2,1)}, u32[]{:S(2)}) copy-start(bf16[128,2048]{1,0:T(8,128)(2,1)} %param.20) | copy-start | bytes 1572868
  61.1 4.9 %copy-start.8 = (f32[2048]{0:T(1024)S(1)}, f32[2048]{0:T(1024)}, u32[]{:S(2)}) copy-start(f32[2048]{0:T(1024)} %param.22) | copy-start | bytes 24580
  61.1 5.9 %copy-start.5 = (bf16[2048,16]{0,1:T(8,128)(2,1)S(1)}, bf16[2048,16]{0,1:T(8,128)(2,1)}, u32[]{:S(2)}) copy-start(bf16[2048,16]{0,1:T(8,128)(2,1)} %param.23) | copy-start | bytes 196612
  61.1 7.2 %copy-start.6 = (s32[128,8]{0,1:T(8,128)S(1)}, s32[128,8]{0,1:T(8,128)}, u32[]{:S(2)}) copy-start(s32[128,8]{0,1:T(8,128)} %param.27) | copy-start | bytes 12292
  66.0 89.4 %copy-start.1 = (bf16[128,2048]{1,0:T(8,128)(2,1)}, bf16[128,2048]{1,0:T(8,128)(2,1)S(1)}, u32[]{:S(2)}) copy-start(bf16[128,2048]{1,0:T(8,128)(2,1)S(1)} %get-tuple-element.13) | copy-start | bytes 1572868
  67.0 216.5 %reduce-scatter.2.cloned.1.call-start = ((), (), s32[]{:S(2)}) async-start(), calls=%async_computation.4 | async-start | bytes 8912896 | tf_op jit(solution)/shard_map/reduce_scatter | solution.py:134
Sparse Core Ops, SparseCore 0:
  9.6 22.5 all-gather.2
  67.1 73.7 all-gather.4
  181.5 102.0 reduce-scatter.1
where the time goes:
time: 290 us
  waiting for transfers between devices  168 us (58%)
  matrix products  54.9 us (19%)
  blocking collectives  37.9 us (13%)
  between operations  16 us (6%)
  starting transfers between devices  7.95 us (3%)
  other arithmetic  3.09 us (1%)
    reduce_scatter x1, waiting for transfers between devices, shards(): lax.psum_scatter(partial.astype(jnp.bfloat16), spread, scatter_dimension=...  102 us
    all_gather x1, waiting for transfers between devices, shards(): all_rows = lax.all_gather(normed, spread, axis=0, tiled=True)  51.7 us
    dot_general x1, matrix products, run_expert(): answer = jnp.dot(activated, w_down, preferred_element_type=jnp.float32)  26 us
    all_gather x1, blocking collectives, shards(): all_gates = lax.all_gather(dense_gates, spread, axis=0, tiled=True)  20.6 us
    dot_general x1, matrix products, run_expert(): gate_pre = jnp.dot(rows, w_gate, preferred_element_type=jnp.float32)  14.4 us
    unnamed x1, blocking collectives  13.1 us
    ppermute x2, waiting for transfers between devices, carried_in(): lax.ppermute(window.astype(jnp.bfloat16), 'seq', [(i, i + span) for i in...  12.9 us
    ppermute x2, starting transfers between devices, carried_in(): lax.ppermute(window.astype(jnp.bfloat16), 'seq', [(i, i + span) for i in...  7.83 us
  transfers between devices with their start and end apart: 5, of which 4 were waited for; matrix products, arithmetic and copies ran while one was open for 5% of the time, Pallas kernels for 0%

commit v1 on v0

--- a/solution.py
+++ b/solution.py
@@ -123,7 +123,9 @@
     gate_weights = gates / jnp.sum(gates, axis=1, keepdims=True)
     dense_gates = jnp.sum(jnp.where(picked, gate_weights[:, :, None], 0.0), axis=1)
     spread = ("seq", "head")
-    all_rows = lax.all_gather(normed, spread, axis=0, tiled=True)
+    all_rows = jnp.concatenate(
+        lax.all_to_all(jnp.stack([normed] * lax.axis_size(spread)), spread, 0, 0), axis=0
+    )
     all_gates = lax.all_gather(dense_gates, spread, axis=0, tiled=True)
     exp_dev = w_gate.shape[0]
     first = (lax.axis_index("seq") * lax.axis_size("head") + lax.axis_index("head")) * exp_dev

time: 290 us -> 419 us (1.44)
  blocking collectives: 37.9 us -> 183 us
  waiting for transfers between devices: 168 us -> 143 us
  starting transfers between devices: 7.95 us -> 12.8 us
  local copies, waits for them, and re-layouts: 2.73 us -> 7.02 us
    all_gather x1, blocking collectives: 20.6 us -> 166 us  [shards(): all_gates = lax.all_gather(dense_gates, spread, axis=0, tiled=True)]
    all_gather x1 -> x0, waiting for transfers between devices: 51.7 us -> none  [shards(): all_rows = lax.all_gather(normed, spread, axis=0, tiled=True)]
    reduce_scatter x1, waiting for transfers between devices: 102 us -> 130 us  [shards(): lax.psum_scatter(partial.astype(jnp.bfloat16), spread, scatter_dimension=...]
    all_to_all x0 -> x1, starting transfers between devices: none -> 4.87 us  [shards(): lax.all_to_all(jnp.stack([normed] * lax.axis_size(spread)), spread, 0, 0)]
    another operation x0 -> x1, local copies, waits for them, and re-layouts: none -> 4.28 us  [shards(): jnp.stack([normed] * lax.axis_size(spread))]
  transfers between devices with their start and end apart: 5 -> 5, of which waited for: 4 -> 3; matrix products, arithmetic and copies ran while one was open for 5% -> 3% of each run, Pallas kernels for 0% -> 0%
where the time goes in v1:
time: 419 us; the launch traced here: 418 us
  blocking collectives  183 us (44%)
  waiting for transfers between devices  143 us (34%)
  matrix products  53.8 us (13%)
  between operations  16.3 us (4%)
  starting transfers between devices  12.8 us (3%)
  local copies, waits for them, and re-layouts  7.02 us (2%)
    all_gather x1, blocking collectives, shards(): all_gates = lax.all_gather(dense_gates, spread, axis=0, tiled=True)  166 us
    reduce_scatter x1, waiting for transfers between devices, shards(): lax.psum_scatter(partial.astype(jnp.bfloat16), spread, scatter_dimension=...  130 us
    dot_general x1, matrix products, run_expert(): answer = jnp.dot(activated, w_down, preferred_element_type=jnp.float32)  26 us
    dot_general x1, matrix products, run_expert(): gate_pre = jnp.dot(rows, w_gate, preferred_element_type=jnp.float32)  14.4 us
    unnamed x1, blocking collectives  13.1 us
    ppermute x2, waiting for transfers between devices, carried_in(): lax.ppermute(window.astype(jnp.bfloat16), 'seq', [(i, i + span) for i in...  12.9 us
  transfers between devices with their start and end apart: 5, of which 3 were waited for; matrix products, arithmetic and copies ran while one was open for 3% of the time, Pallas kernels for 0%

profile of v1, /device:TPU:0, one launch (start us, length us, event | category | flops | bytes accessed | tf_op | source)
XLA Modules:
  0.0 418.5 jit_solution(3478359760909114407)
XLA Ops:
  7.3 0.7 all-gather.2.cloned.1.call-update
  8.0 0.6 dynamic-slice
  8.6 1.2 slice_dynamic-update-slice_fusion
  9.8 13.1 %all-reduce = s32[8]{0:T(128)S(1)} all-reduce(s32[8]{0:T(128)S(1)} %get-tuple-element.4), channel_id=1, replica_groups=mesh['groups'=2,'seq'=8,'head'=2] {'seq'}, use_global_device_ids=true, to_apply=%add | all-reduce | flops 8 | bytes 64
  22.9 0.6 fusion.43
  24.2 0.7 compare_convert_fusion.1
  24.9 1.1 fusion.12
  26.0 1.2 fusion.44
  27.2 3.4 collective-permute-start
  31.3 7.9 %collective-permute-done = bf16[8,256,128]{2,1,0:T(8,128)(2,1)S(1)} collective-permute-done((bf16[8,256,128]{2,1,0:T(8,128)(2,1)}, bf16[8,256,128]{2,1,0:T(8,128)(2,1)S(1)}, u32[]{:S(2)}, u32[]{:S(2)}) %collective-permute-start) | collective-permute-done | bytes 524320 | tf_op jit(solution)/shard_map/ppermute | solution.py:24
  39.3 0.9 fusion.18
  40.2 4.4 %collective-permute-start.1 = (bf16[8,256,128]{2,1,0:T(8,128)(2,1)}, bf16[8,256,128]{2,1,0:T(8,128)(2,1)S(1)}, u32[]{:S(2)}, u32[]{:S(2)}) collective-permute-start(bf16[8,256,128]{2,1,0:T(8,128)(2,1)} %fusion.18), channel_id=1, source_target_pairs={{0,4},{2,6},{4,8},{6,10},{8,12},{10,14},{1,5},{3,7},{5,9},{7,11},{... | collective-permute-start | bytes 1572872 | tf_op jit(solution)/shard_map/ppermute | solution.py:24
  45.3 2.2 fusion.9
  47.5 5.0 %collective-permute-done.1 = bf16[8,256,128]{2,1,0:T(8,128)(2,1)S(1)} collective-permute-done((bf16[8,256,128]{2,1,0:T(8,128)(2,1)}, bf16[8,256,128]{2,1,0:T(8,128)(2,1)S(1)}, u32[]{:S(2)}, u32[]{:S(2)}) %collective-permute-start.1) | collective-permute-done | bytes 524320 | tf_op jit(solution)/shard_map/ppermute | solution.py:24
  52.5 1.4 fusion.16
  54.0 2.5 multiply_reduce_fusion
  56.9 4.2 all_to_all.21
  61.1 4.8 %fusion.20 = (f32[128]{0:T(128)S(1)}, bf16[128,2048]{1,0:T(8,128)(2,1)S(1)}) fusion(bf16[128,2048]{0,1:T(8,128)(2,1)S(1)} %bitcast.72, bf16[2048,2048]{1,0:T(8,128)(2,1)} %all-gather.2.cloned.1.call-done, bf16[128,2048]{1,0:T(8,128)(2,1)S(1)} %copy-done.4), kind=kOutput, calls=%fused_computation.32 | convolution fusion | flops 1075314560 | bytes 9961984 | tf_op jit(solution)/shard_map/dot_general | solution.py:105
  66.1 4.3 %stack.2 = bf16[16,128,2048]{2,1,0:T(8,128)(2,1)} broadcast(bf16[128,2048]{1,0:T(8,128)(2,1)S(1)} %fusion.22), dimensions={1,2} | broadcast | bytes 8912896 | tf_op jit(solution)/shard_map/stack | solution.py:127
  70.4 4.9 %all-to-all-start.1 = ((bf16[16,128,2048]{2,1,0:T(8,128)(2,1)}), bf16[16,128,2048]{2,1,0:T(8,128)(2,1)}, u32[]{:S(2)}, u32[]{:S(2)}) async-start(bf16[16,128,2048]{2,1,0:T(8,128)(2,1)} %stack.2), calls=%async_computation.1 | async-start | bytes 16777216 | tf_op jit(solution)/shard_map/all_to_all | solution.py:127
  75.7 165.5 %all_gather.11 = f32[2048,16]{0,1:T(8,128)S(1)} all-gather(f32[128,16]{0,1:T(8,128)S(1)} %select_reduce_fusion.1), channel_id=1, replica_groups=mesh['groups'=2,'seq'=8,'head'=2] {'seq','head'}, dimensions={0}, use_global_device_ids=true | all-gather | bytes 139264 | tf_op jit(solution)/shard_map/all_gather | solution.py:129
  241.3 14.4 %fusion.3 = f32[2048,1024]{1,0:T(8,128)} fusion(bf16[2048,2048]{1,0:T(8,128)(2,1)} %bitcast.11, bf16[1,2048,1024]{2,1,0:T(8,128)(2,1)} %param.24), kind=kOutput, calls=%fused_computation.8 | convolution fusion | flops 8589934592 | bytes 20971520 | tf_op jit(solution)/shard_map/dot_general | solution.py:45
  255.8 26.0 %multiply_convert_fusion = bf16[2048,2048]{1,0:T(8,128)(2,1)} fusion(f32[2048]{0:T(1024)S(1)} %select_reduce_fusion, f32[2048,1024]{1,0:T(8,128)} %fusion.3, bf16[2048,2048]{1,0:T(8,128)(2,1)} %bitcast.11, bf16[1,1024,2048]{2,1,0:T(8,128)(2,1)} %param.26, bf16[1,2048,1024]{2,1,0:T(8,128)(2,1)} %param.25), kind=kOutput, calls=%fused_computation | convolution fusion | flops 17200840704 | bytes 33562624 | tf_op jit(solution)/shard_map/dot_general | solution.py:48
  281.8 129.9 %reduce-scatter.2.cloned.1.call-done = bf16[128,2048]{1,0:T(8,128)(2,1)} async-done(((bf16[2048,2048]{1,0:T(8,128)(2,1)}), bf16[128,2048]{1,0:T(8,128)(2,1)}) %reduce-scatter.2.cloned.1.call-update) | async-done | bytes 524304 | tf_op jit(solution)/shard_map/reduce_scatter | solution.py:136
  (46 shorter events, 1.3 us)
Async XLA Ops:
  7.2 17.7 %copy-start = (bf16[8,128,256]{2,1,0:T(8,128)(2,1)S(1)}, bf16[8,128,256]{2,1,0:T(8,128)(2,1)}, u32[]{:S(2)}) copy-start(bf16[8,128,256]{2,1,0:T(8,128)(2,1)} %param.18) | copy-start | bytes 1572868
  7.2 0.8 copy-start.12
  7.2 1.4 copy-start.8
  7.2 17.7 %copy-start.11 = (bf16[256,1024]{1,0:T(8,128)(2,1)S(1)}, bf16[256,1024]{1,0:T(8,128)(2,1)}, u32[]{:S(2)}) copy-start(bf16[256,1024]{1,0:T(8,128)(2,1)} %param.15) | copy-start | bytes 1572868
  7.2 18.8 %copy-start.5 = (bf16[256,1024]{1,0:T(8,128)(2,1)S(1)}, bf16[256,1024]{1,0:T(8,128)(2,1)}, u32[]{:S(2)}) copy-start(bf16[256,1024]{1,0:T(8,128)(2,1)} %param.16) | copy-start | bytes 1572868
  7.2 53.9 %all-gather.2.cloned.1.call-start = ((), (), s32[]{:S(2)}) async-start(), calls=%async_computation.3 | async-start | bytes 12582912 | tf_op jit(solution)/shard_map/all_gather | solution.py:107
  27.2 12.0 %collective-permute-start = (bf16[8,256,128]{2,1,0:T(8,128)(2,1)}, bf16[8,256,128]{2,1,0:T(8,128)(2,1)S(1)}, u32[]{:S(2)}, u32[]{:S(2)}) collective-permute-start(bf16[8,256,128]{2,1,0:T(8,128)(2,1)} %get-tuple-element.8), channel_id=1, source_target_pairs={{0,2},{2,4},{4,6},{6,8},{8,10},{10,12},{12,14},{1,3},{3,5},{5,7},{... | collective-permute-start | bytes 1572872 | tf_op jit(solution)/shard_map/ppermute | solution.py:24
  40.2 12.3 %collective-permute-start.1 = (bf16[8,256,128]{2,1,0:T(8,128)(2,1)}, bf16[8,256,128]{2,1,0:T(8,128)(2,1)S(1)}, u32[]{:S(2)}, u32[]{:S(2)}) collective-permute-start(bf16[8,256,128]{2,1,0:T(8,128)(2,1)} %fusion.18), channel_id=1, source_target_pairs={{0,4},{2,6},{4,8},{6,10},{8,12},{10,14},{1,5},{3,7},{5,9},{7,11},{... | collective-permute-start | bytes 1572872 | tf_op jit(solution)/shard_map/ppermute | solution.py:24
  47.5 5.0 %copy-start.3 = (bf16[256,8,256]{0,2,1:T(8,128)(2,1)}, bf16[256,8,256]{0,2,1:T(8,128)(2,1)S(1)}, u32[]{:S(2)}) copy-start(bf16[256,8,256]{0,2,1:T(8,128)(2,1)S(1)} %fusion.9) | copy-start | bytes 3145732
  47.5 9.0 %copy-start.10 = (f32[1024]{0:T(1024)S(1)}, f32[1024]{0:T(1024)}, u32[]{:S(2)}) copy-start(f32[1024]{0:T(1024)} %param.19) | copy-start | bytes 12292
  54.0 7.1 %copy-start.4 = (bf16[128,2048]{1,0:T(8,128)(2,1)S(1)}, bf16[128,2048]{1,0:T(8,128)(2,1)}, u32[]{:S(2)}) copy-start(bf16[128,2048]{1,0:T(8,128)(2,1)} %param.20) | copy-start | bytes 1572868
  61.1 4.8 %copy-start.9 = (f32[2048]{0:T(1024)S(1)}, f32[2048]{0:T(1024)}, u32[]{:S(2)}) copy-start(f32[2048]{0:T(1024)} %param.22) | copy-start | bytes 24580
  65.9 4.5 %copy-start.2 = (bf16[128,2048]{1,0:T(8,128)(2,1)}, bf16[128,2048]{1,0:T(8,128)(2,1)S(1)}, u32[]{:S(2)}) copy-start(bf16[128,2048]{1,0:T(8,128)(2,1)S(1)} %get-tuple-element.13) | copy-start | bytes 1572868
  70.4 5.0 %copy-start.6 = (bf16[2048,16]{0,1:T(8,128)(2,1)S(1)}, bf16[2048,16]{0,1:T(8,128)(2,1)}, u32[]{:S(2)}) copy-start(bf16[2048,16]{0,1:T(8,128)(2,1)} %param.23) | copy-start | bytes 196612
  70.4 5.2 %copy-start.7 = (s32[128,8]{0,1:T(8,128)S(1)}, s32[128,8]{0,1:T(8,128)}, u32[]{:S(2)}) copy-start(s32[128,8]{0,1:T(8,128)} %param.27) | copy-start | bytes 12292
  70.4 171.0 %all-to-all-start.1 = ((bf16[16,128,2048]{2,1,0:T(8,128)(2,1)}), bf16[16,128,2048]{2,1,0:T(8,128)(2,1)}, u32[]{:S(2)}, u32[]{:S(2)}) async-start(bf16[16,128,2048]{2,1,0:T(8,128)(2,1)} %stack.2), calls=%async_computation.1 | async-start | bytes 16777216 | tf_op jit(solution)/shard_map/all_to_all | solution.py:127
  75.3 336.4 %reduce-scatter.2.cloned.1.call-start = ((), (), s32[]{:S(2)}) async-start(), calls=%async_computation.4 | async-start | bytes 8912896 | tf_op jit(solution)/shard_map/reduce_scatter | solution.py:136
  281.7 129.9 %copy-start.1 = (bf16[8,128,256]{2,1,0:T(8,128)(2,1)S(1)}, bf16[8,128,256]{2,1,0:T(8,128)(2,1)}, u32[]{:S(2)}) copy-start(bf16[8,128,256]{2,1,0:T(8,128)(2,1)} %param.18) | copy-start | bytes 1572868
Sparse Core Ops, SparseCore 0:
  9.6 22.5 all-gather.1
  281.9 129.6 reduce-scatter.1
